TPU v7x, 32 devices: a whole 2x2x4 slice. The times are simulated.
32 devices in a mesh: member: 8 (over y, x, core), lat: 4 (over z).
Axes of the slice: x: 2, y: 2, z: 4, core: 2. Of those that a mesh axis runs over, the one named last changes fastest.
Arguments:
- state: float32 [32, 32, 8, 256], P('member', 'lat'), may hold values from -6 to 6
- zonal_wind: float32 [32, 8, 256], P('lat'), may hold values from -5 to 5
- meridional_wind: float32 [32, 8, 256], P('lat'), may hold values from -5 to 5
- obs_cell: int32 [32, 8, 128], P('lat'), may hold values from 0 to 255
- obs_value: float32 [32, 8, 128], P('lat'), may hold values from -10 to 10
- obs_weight: float32 [32, 8, 128], P('lat'), may hold values from 1 to 1024
Outputs:
- analysis: float32 [32, 32, 8, 256], P('member', 'lat')
All inputs are finite; a program needn't handle non-finite values.
Results may differ from a plain program's by a relative error of at most 0.00014.
Values sent between devices are 32-bit elements; how exact they have to be, the bound alone decides.
No kernel may reach another device: no remote copies, remote signals or barrier semaphores. Data moves between devices by JAX's collectives and lax.ppermute only.
A program may use at most 64 MiB of HBM per device.

v0:
```python
import jax
import jax.numpy as jnp
from jax import lax
from jax.sharding import PartitionSpec as P

SWEEPS = 3
step_size = 0.3


def extended_2(block, sides, width):
    for axis, dim in sides:
        count = lax.axis_size(axis)
        forward = [(i, i + 1) for i in range(count - 1)]
        backward = [(target, source) for source, target in forward]
        low = lax.ppermute(
            lax.slice_in_dim(block, block.shape[dim] - width, None, axis=dim), axis, forward
        )
        high = lax.ppermute(lax.slice_in_dim(block, 0, width, axis=dim), axis, backward)
        block = jnp.concatenate([low, block, high], axis=dim)
    return block


def advance(padded, zonal, meridional):
    middle = padded[:, 1:-1]
    north_row = padded[:, 2:]
    south_row = padded[:, :-2]
    east_cell = jnp.roll(middle, -1, axis=3)
    west_cell = jnp.roll(middle, 1, axis=3)
    return middle - step_size * (
        (zonal + middle) * (east_cell - west_cell) * 0.5
        + meridional * (north_row - south_row) * 0.5
    )


def analyse(ensemble, observed, values, weights):
    highest = lax.Precision.HIGHEST
    count = ensemble.shape[0]
    obs_mean = jnp.mean(observed, axis=0)
    perturb = observed - obs_mean
    innovation = values - obs_mean
    gram = jnp.einsum("kro,lro->rkl", perturb * weights, perturb, precision=highest)
    identity = jnp.eye(count, dtype=jnp.float32)
    system = gram + (count - 1.0) * identity
    frobenius = jnp.sqrt(jnp.sum(system * system, axis=(1, 2)))
    iterate = system / frobenius[:, None, None]
    inverse = jnp.broadcast_to(identity, system.shape)
    for sweep in range(SWEEPS):
        product = jnp.einsum("rij,rjk->rik", inverse, iterate, precision=highest)
        factor = 1.5 * identity - 0.5 * product
        iterate = jnp.einsum("rij,rjk->rik", iterate, factor, precision=highest)
        inverse = jnp.einsum("rij,rjk->rik", factor, inverse, precision=highest)
    root = inverse / jnp.sqrt(frobenius)[:, None, None]
    covariance = jnp.einsum("rij,rjk->rik", root, root, precision=highest)
    projected = jnp.einsum("kro,ro->rk", perturb, weights * innovation, precision=highest)
    mean_weights = jnp.einsum("rkl,rl->rk", covariance, projected, precision=highest)
    transform = mean_weights[:, :, None] + jnp.sqrt(count - 1.0) * root
    state_mean = jnp.mean(ensemble, axis=0)
    state_pert = ensemble - state_mean
    return state_mean + jnp.einsum("rkm,krn->mrn", transform, state_pert, precision=highest)


def pick_columns(rows, cells):
    return jax.vmap(
        lambda block, index: jnp.take(block, index, axis=1), in_axes=(1, 0), out_axes=1
    )(rows, cells)


def body(state, zonal_wind, meridional_wind, obs_cell, obs_value, obs_weight):
    members_dev, lat_dev, levels, longitudes = state.shape
    groups = lax.axis_size("member")
    regions = lat_dev * levels // groups
    count = members_dev * groups
    stacked = jnp.concatenate([state, zonal_wind[None], meridional_wind[None]], axis=0)
    extended = extended_2(stacked, (("lat", 1),), 2)
    first = advance(
        extended[:members_dev], extended[members_dev, 1:-1], extended[members_dev + 1, 1:-1]
    )
    field = advance(first, zonal_wind, meridional_wind)
    flat = field.reshape(members_dev, lat_dev * levels, longitudes)
    all_cells = obs_cell.reshape(lat_dev * levels, -1)
    start = lax.axis_index("member") * regions
    cells = lax.dynamic_slice_in_dim(all_cells, start, regions, 0)
    values = lax.dynamic_slice_in_dim(obs_value.reshape(lat_dev * levels, -1), start, regions, 0)
    weights = lax.dynamic_slice_in_dim(obs_weight.reshape(lat_dev * levels, -1), start, regions, 0)
    ensemble = lax.all_to_all(
        flat.reshape(members_dev, groups, regions, longitudes),
        "member",
        split_axis=1,
        concat_axis=0,
        tiled=True,
    ).reshape(count, regions, longitudes)
    observed = pick_columns(ensemble, cells)
    analysed = analyse(ensemble, observed, values, weights)
    returned = lax.all_to_all(
        analysed.reshape(count, 1, regions, longitudes),
        "member",
        split_axis=0,
        concat_axis=1,
        tiled=True,
    )
    return returned.reshape(state.shape)


def solution(mesh):
    in_specs = (
        P("member", "lat", None, None),
        P("lat", None, None),
        P("lat", None, None),
        P("lat", None, None),
        P("lat", None, None),
        P("lat", None, None),
    )
    out_specs = P("member", "lat", None, None)
    return jax.shard_map(body, mesh=mesh, in_specs=in_specs, out_specs=out_specs, check_vma=False)
```

profile of v0, /device:TPU:0, one launch (start us, length us, event | category | flops | bytes accessed | tf_op | source)
XLA Modules:
  0.0 47.4 jit_solution(7783131057567353832)
XLA Ops:
  0.0 1.0 %pad_maximum_fusion.7 = (f32[6,2,8,256]{3,2,0,1:T(8,128)S(1)}, f32[6,2,8,256]{3,2,0,1:T(8,128)S(1)}) fusion(f32[1,8,8,256]{3,2,0,1:T(8,128)} %bitcast.75, f32[1,8,8,256]{3,2,0,1:T(8,128)} %bitcast.79, f32[4,8,8,256]{3,2,1,0:T(8,128)} %param.6), kind=kLoop, calls=%fused_computation.45 | loop fusion | flops 98304 | bytes 589824 | tf_op jit(solution)/shard_map/concatenate | solution.py:73
  1.0 5.0 %collective-permute-start = (f32[6,2,8,256]{3,2,0,1:T(8,128)S(1)}, f32[6,2,8,256]{3,2,0,1:T(8,128)S(1)}, u32[]{:S(2)}, u32[]{:S(2)}) collective-permute-start(f32[6,2,8,256]{3,2,0,1:T(8,128)S(1)} %get-tuple-element.12), channel_id=1, source_target_pairs={{0,1},{1,2},{2,3},{4,5},{5,6},{6,7},{8,9},{9,10},{10,11},{12,13},{... | collective-permute-start | bytes 294920 | tf_op jit(solution)/shard_map/ppermute | solution.py:15
  6.0 1.3 %collective-permute-start.1 = (f32[6,2,8,256]{3,2,0,1:T(8,128)S(1)}, f32[6,2,8,256]{3,2,0,1:T(8,128)S(1)}, u32[]{:S(2)}, u32[]{:S(2)}) collective-permute-start(f32[6,2,8,256]{3,2,0,1:T(8,128)S(1)} %get-tuple-element.11), channel_id=1, source_target_pairs={{1,0},{2,1},{3,2},{5,4},{6,5},{7,6},{9,8},{10,9},{11,10},{13,12},{... | collective-permute-start | bytes 294920 | tf_op jit(solution)/shard_map/ppermute | solution.py:18
  7.3 0.7 %fusion.37 = s32[1024]{0:T(1024)S(1)} fusion(s32[64,128]{1,0:T(8,128)} %bitcast.87, s32[]{:T(128)S(6)} %select_n.18), kind=kLoop, calls=%fused_computation.70 | loop fusion | flops 8192 | bytes 8196 | tf_op jit(solution)/shard_map/vmap(jit(_take))/gather | solution.py:64
  8.2 4.3 %collective-permute-done.1 = f32[6,2,8,256]{3,2,0,1:T(8,128)S(1)} collective-permute-done((f32[6,2,8,256]{3,2,0,1:T(8,128)S(1)}, f32[6,2,8,256]{3,2,0,1:T(8,128)S(1)}, u32[]{:S(2)}, u32[]{:S(2)}) %collective-permute-start.1) | collective-permute-done | bytes 98336 | tf_op jit(solution)/shard_map/ppermute | solution.py:18
  13.4 0.9 %fusion.13 = f32[4,8,8,256]{3,2,0,1:T(8,128)} fusion(f32[4,10,8,256]{3,2,0,1:T(8,128)S(1)} %fusion.8, f32[4,8,8,1]{3,2,0,1:T(8,128)S(1)} %get-tuple-element.14, f32[4,8,8,255]{3,2,0,1:T(8,128)S(1)} %get-tuple-element.16, f32[4,8,8,255]{3,2,0,1:T(8,128)S(1)} %get-tuple-element.15, f32[4,8,8,1]{3,2,0,1:T(8,128)S(1)} %get-tuple-element.13, ...), kind=kLoop, calls=%fused_computation.30 | loop fusion | flops 655360 | bytes 1703936 | tf_op jit(solution)/shard_map/sub | solution.py:29
  14.3 3.7 %all-to-all-start = ((f32[4,8,8,256]{3,2,0,1:T(8,128)}), f32[4,8,8,256]{3,2,0,1:T(8,128)S(1)}, u32[]{:S(2)}, u32[]{:S(2)}) async-start(f32[4,8,8,256]{3,2,0,1:T(8,128)} %fusion.13), calls=%async_computation | async-start | bytes 524288 | tf_op jit(solution)/shard_map/all_to_all | solution.py:85
  18.0 0.7 %compare_and_fusion = pred[8,128]{1,0:T(8,128)(4,1)S(1)} fusion(s32[64,128]{1,0:T(8,128)} %bitcast.88, s32[]{:T(128)S(6)} %select_n.18), kind=kLoop, calls=%fused_computation.73 | loop fusion | flops 6144 | bytes 5124 | tf_op jit(solution)/shard_map/vmap(jit(_take))/and | solution.py:64
  18.7 6.2 %all-to-all-done = f32[4,8,8,256]{3,2,0,1:T(8,128)S(1)} async-done(((f32[4,8,8,256]{3,2,0,1:T(8,128)}), f32[4,8,8,256]{3,2,0,1:T(8,128)S(1)}, u32[]{:S(2)}, u32[]{:S(2)}) %all-to-all-start) | async-done | bytes 262176 | tf_op jit(solution)/shard_map/all_to_all | solution.py:85
  24.9 0.4 copy.19
  25.3 6.8 %gather_fusion = f32[1024,32]{1,0:T(8,128)S(1)} fusion(f32[8,32,256]{1,2,0:T(8,128)S(1)} %bitcast.74, s32[1024]{0:T(1024)S(1)} %fusion.37), kind=kCustom, calls=%fused_computation | custom fusion | bytes 270336 | tf_op jit(solution)/shard_map/vmap(jit(_take))/gather | solution.py:64
  32.3 0.7 %subtract_multiply_fusion = (f32[8,128]{1,0:T(8,128)S(1)}, f32[8,128]{1,0:T(8,128)S(1)}, f32[8,128]{1,0:T(8,128)S(1)}) fusion(f32[64,128]{1,0:T(8,128)} %bitcast.89, s32[]{:T(128)S(6)} %select_n.18, f32[64,128]{1,0:T(8,128)} %bitcast.90, f32[8,128]{1,0:T(8,128)S(1)} %bitcast_reduce_fusion.1), kind=kLoop, calls=%fused_computation.71 | loop fusion | flops 3072 | bytes 24580 | tf_op jit(solution)/shard_map/mul | solution.py:54
  33.0 0.4 multiply_reduce_fusion
  33.4 0.3 fusion.3
  33.8 0.3 fusion.33
  34.1 0.3 fusion.28
  34.4 0.3 fusion.2
  35.2 0.3 convolution_bitcast_fusion
  35.5 0.3 fusion.1
  35.7 0.3 convolution_divide_fusion
  36.3 0.3 fusion.48
  36.7 0.5 %fusion = f32[32,1,8,256]{3,0,2,1:T(8,128)S(1)} fusion(f32[32,8,256]{2,1,0:T(8,128)S(1)} %broadcast_subtract_fusion, f32[8,32,32]{2,1,0:T(8,128)S(1)} %convolution_divide_fusion, f32[8,256]{1,0:T(8,128)S(1)} %broadcast_multiply_fusion, f32[8,32]{1,0:T(8,128)S(1)} %bitcast.85), kind=kOutput, calls=%fused_computation.2 | convolution fusion | flops 25247744 | bytes 566272 | tf_op jit(solution)/shard_map/rkm,krn->mrn/dot_general | solution.py:59
  37.3 9.3 %all_to_all.33 = f32[32,1,8,256]{3,2,1,0:T(8,128)S(1)} all-to-all(f32[32,1,8,256]{3,2,1,0:T(8,128)S(1)} %copy.23), channel_id=1, replica_groups=mesh['member'=8,'lat'=4] {'member'}, dimensions={0} | all-to-all | bytes 524288 | tf_op jit(solution)/shard_map/all_to_all | solution.py:94
  46.7 0.7 %copy.41 = f32[8,4,1,8,256]{4,3,0,1,2:T(8,128)} copy(f32[8,4,1,8,256]{4,3,1,0,2:T(8,128)S(1)} %bitcast.83) | data formatting | bytes 524288 | tf_op jit(solution)/shard_map/all_to_all | solution.py:94
  (27 shorter events, 2.2 us)
Async XLA Ops:
  0.0 12.5 %copy-start = (f32[4,8,8,256]{3,2,1,0:T(8,128)S(1)}, f32[4,8,8,256]{3,2,1,0:T(8,128)}, u32[]{:S(2)}) copy-start(f32[4,8,8,256]{3,2,1,0:T(8,128)} %param.6) | copy-start | bytes 786436
  0.0 12.5 %copy-start.1 = (f32[8,8,256]{2,1,0:T(8,128)S(1)}, f32[8,8,256]{2,1,0:T(8,128)}, u32[]{:S(2)}) copy-start(f32[8,8,256]{2,1,0:T(8,128)} %param.8) | copy-start | bytes 196612
  0.0 12.5 %copy-start.2 = (f32[8,8,256]{2,1,0:T(8,128)S(1)}, f32[8,8,256]{2,1,0:T(8,128)}, u32[]{:S(2)}) copy-start(f32[8,8,256]{2,1,0:T(8,128)} %param.7) | copy-start | bytes 196612
  1.0 7.2 %collective-permute-start = (f32[6,2,8,256]{3,2,0,1:T(8,128)S(1)}, f32[6,2,8,256]{3,2,0,1:T(8,128)S(1)}, u32[]{:S(2)}, u32[]{:S(2)}) collective-permute-start(f32[6,2,8,256]{3,2,0,1:T(8,128)S(1)} %get-tuple-element.12), channel_id=1, source_target_pairs={{0,1},{1,2},{2,3},{4,5},{5,6},{6,7},{8,9},{9,10},{10,11},{12,13},{... | collective-permute-start | bytes 294920 | tf_op jit(solution)/shard_map/ppermute | solution.py:15
  6.0 6.5 %collective-permute-start.1 = (f32[6,2,8,256]{3,2,0,1:T(8,128)S(1)}, f32[6,2,8,256]{3,2,0,1:T(8,128)S(1)}, u32[]{:S(2)}, u32[]{:S(2)}) collective-permute-start(f32[6,2,8,256]{3,2,0,1:T(8,128)S(1)} %get-tuple-element.11), channel_id=1, source_target_pairs={{1,0},{2,1},{3,2},{5,4},{6,5},{7,6},{9,8},{10,9},{11,10},{13,12},{... | collective-permute-start | bytes 294920 | tf_op jit(solution)/shard_map/ppermute | solution.py:18
  14.3 10.6 %all-to-all-start = ((f32[4,8,8,256]{3,2,0,1:T(8,128)}), f32[4,8,8,256]{3,2,0,1:T(8,128)S(1)}, u32[]{:S(2)}, u32[]{:S(2)}) async-start(f32[4,8,8,256]{3,2,0,1:T(8,128)} %fusion.13), calls=%async_computation | async-start | bytes 524288 | tf_op jit(solution)/shard_map/all_to_all | solution.py:85
where the time goes:
time: 47.8 us; the launch traced here: 47.4 us
  waiting for transfers between devices  10.7 us (22%)
  starting transfers between devices  9.98 us (21%)
  blocking collectives  9.32 us (19%)
  local copies, waits for them, and re-layouts  8.71 us (18%)
  other arithmetic  4.47 us (9%)
  matrix products  4.01 us (8%)
    all_to_all x1, blocking collectives, body(): lax.all_to_all(analysed.reshape(count, 1, regions, longitudes), 'member',...  9.32 us
    gather x2, local copies, waits for them, and re-layouts, pick_columns(): jnp.take(block, index, axis=1)  6.96 us
    all_to_all x1, waiting for transfers between devices, body(): lax.all_to_all(flat.reshape(members_dev, groups, regions, longitudes), 'm...  6.19 us
    ppermute x1, starting transfers between devices, extended_2(): lax.ppermute(lax.slice_in_dim(block, block.shape[dim] - width, None, axis...  4.97 us
    ppermute x1, waiting for transfers between devices, extended_2(): lax.ppermute(lax.slice_in_dim(block, 0, width, axis=dim), axis, backward)  4.32 us
    all_to_all x1, starting transfers between devices, body(): lax.all_to_all(flat.reshape(members_dev, groups, regions, longitudes), 'm...  3.72 us
    ppermute x1, starting transfers between devices, extended_2(): lax.ppermute(lax.slice_in_dim(block, 0, width, axis=dim), axis, backward)  1.29 us
    sub x2, other arithmetic, advance(): middle - step_size * ((zonal + middle) * (east_cell - west_cell) * 0.5 +...  1.16 us
  transfers between devices with their start and end apart: 3, of which 3 were waited for; matrix products, arithmetic and copies ran while one was open for 3% of the time, Pallas kernels for 0%

commit v1 on v0

--- a/solution.py
+++ b/solution.py
@@ -5,6 +5,13 @@
 
 SWEEPS = 3
 step_size = 0.3
+
+
+def trade_parts(x, axis, split, join):
+    size = lax.axis_size(axis)
+    blocks = jnp.stack(jnp.split(x, size, axis=split), axis=0)
+    blocks = lax.all_to_all(blocks, axis, split_axis=0, concat_axis=0)
+    return jnp.concatenate(blocks, axis=join)
 
 
 def extended_2(block, sides, width):
@@ -82,12 +89,8 @@
     cells = lax.dynamic_slice_in_dim(all_cells, start, regions, 0)
     values = lax.dynamic_slice_in_dim(obs_value.reshape(lat_dev * levels, -1), start, regions, 0)
     weights = lax.dynamic_slice_in_dim(obs_weight.reshape(lat_dev * levels, -1), start, regions, 0)
-    ensemble = lax.all_to_all(
-        flat.reshape(members_dev, groups, regions, longitudes),
-        "member",
-        split_axis=1,
-        concat_axis=0,
-        tiled=True,
+    ensemble = trade_parts(
+        flat.reshape(members_dev, groups, regions, longitudes), "member", 1, 0
     ).reshape(count, regions, longitudes)
     observed = pick_columns(ensemble, cells)
     analysed = analyse(ensemble, observed, values, weights)

time: 47.8 us -> 52 us (1.088)
  local copies, waits for them, and re-layouts: 8.71 us -> 13.6 us
  other arithmetic: 4.47 us -> 3.75 us
    unnamed x6 -> x13, local copies, waits for them, and re-layouts: 0.01 us -> 4.33 us
    another operation x0 -> x2, local copies, waits for them, and re-layouts: none -> 0.98 us  [the longest x1 0.62 us: trade_parts(): blocks = jnp.stack(jnp.split(x, size, axis=split), axis=0)]
    sub x2, other arithmetic: 1.16 us -> 0.44 us  [advance(): middle - step_size * ((zonal + middle) * (east_cell - west_cell) * 0.5 +...]
where the time goes in v1:
time: 52 us; the launch traced here: 51.6 us
  local copies, waits for them, and re-layouts  13.6 us (26%)
  waiting for transfers between devices  10.7 us (21%)
  starting transfers between devices  9.98 us (19%)
  blocking collectives  9.32 us (18%)
  matrix products  4 us (8%)
  other arithmetic  3.75 us (7%)
    all_to_all x1, blocking collectives, body(): lax.all_to_all(analysed.reshape(count, 1, regions, longitudes), 'member',...  9.32 us
    gather x2, local copies, waits for them, and re-layouts, pick_columns(): jnp.take(block, index, axis=1)  6.96 us
    all_to_all x1, waiting for transfers between devices, trade_parts(): blocks = lax.all_to_all(blocks, axis, split_axis=0, concat_axis=0)  6.19 us
    ppermute x1, starting transfers between devices, extended_2(): lax.ppermute(lax.slice_in_dim(block, block.shape[dim] - width, None, axis...  4.97 us
    unnamed x13, local copies, waits for them, and re-layouts  4.33 us
    ppermute x1, waiting for transfers between devices, extended_2(): lax.ppermute(lax.slice_in_dim(block, 0, width, axis=dim), axis, backward)  4.32 us
    all_to_all x1, starting transfers between devices, trade_parts(): blocks = lax.all_to_all(blocks, axis, split_axis=0, concat_axis=0)  3.72 us
    ppermute x1, starting transfers between devices, extended_2(): lax.ppermute(lax.slice_in_dim(block, 0, width, axis=dim), axis, backward)  1.29 us
  transfers between devices with their start and end apart: 3, of which 3 were waited for; matrix products, arithmetic and copies ran while one was open for 3% of the time, Pallas kernels for 0%

profile of v1, /device:TPU:0, one launch (start us, length us, event | category | flops | bytes accessed | tf_op | source)
XLA Modules:
  0.0 51.6 jit_solution(10878212042118664636)
XLA Ops:
  0.0 1.0 %pad_maximum_fusion.7 = (f32[6,2,8,256]{3,2,0,1:T(8,128)S(1)}, f32[6,2,8,256]{3,2,0,1:T(8,128)S(1)}) fusion(f32[1,8,8,256]{3,2,0,1:T(8,128)} %bitcast.102, f32[1,8,8,256]{3,2,0,1:T(8,128)} %bitcast.106, f32[4,8,8,256]{3,2,1,0:T(8,128)} %param.6), kind=kLoop, calls=%fused_computation.44 | loop fusion | flops 98304 | bytes 589824 | tf_op jit(solution)/shard_map/concatenate | solution.py:80
  1.0 5.0 %collective-permute-start = (f32[6,2,8,256]{3,2,0,1:T(8,128)S(1)}, f32[6,2,8,256]{3,2,0,1:T(8,128)S(1)}, u32[]{:S(2)}, u32[]{:S(2)}) collective-permute-start(f32[6,2,8,256]{3,2,0,1:T(8,128)S(1)} %get-tuple-element.12), channel_id=1, source_target_pairs={{0,1},{1,2},{2,3},{4,5},{5,6},{6,7},{8,9},{9,10},{10,11},{12,13},{... | collective-permute-start | bytes 294920 | tf_op jit(solution)/shard_map/ppermute | solution.py:22
  6.0 1.3 %collective-permute-start.1 = (f32[6,2,8,256]{3,2,0,1:T(8,128)S(1)}, f32[6,2,8,256]{3,2,0,1:T(8,128)S(1)}, u32[]{:S(2)}, u32[]{:S(2)}) collective-permute-start(f32[6,2,8,256]{3,2,0,1:T(8,128)S(1)} %get-tuple-element.11), channel_id=1, source_target_pairs={{1,0},{2,1},{3,2},{5,4},{6,5},{7,6},{9,8},{10,9},{11,10},{13,12},{... | collective-permute-start | bytes 294920 | tf_op jit(solution)/shard_map/ppermute | solution.py:25
  7.3 0.7 %fusion.45 = s32[1024]{0:T(1024)S(1)} fusion(s32[64,128]{1,0:T(8,128)} %bitcast.114, s32[]{:T(128)S(6)} %select_n.18), kind=kLoop, calls=%fused_computation.85 | loop fusion | flops 8192 | bytes 8196 | tf_op jit(solution)/shard_map/vmap(jit(_take))/gather | solution.py:71
  8.2 4.3 %collective-permute-done.1 = f32[6,2,8,256]{3,2,0,1:T(8,128)S(1)} collective-permute-done((f32[6,2,8,256]{3,2,0,1:T(8,128)S(1)}, f32[6,2,8,256]{3,2,0,1:T(8,128)S(1)}, u32[]{:S(2)}, u32[]{:S(2)}) %collective-permute-start.1) | collective-permute-done | bytes 98336 | tf_op jit(solution)/shard_map/ppermute | solution.py:25
  13.6 0.6 %fusion.40 = f32[8,4,1,8,256]{4,3,1,2,0:T(8,128)} fusion(f32[4,8,8,256]{3,2,0,1:T(8,128)S(1)} %fusion.13), kind=kLoop, calls=%fused_computation.77 | loop fusion | bytes 65536
  14.2 0.6 %fusion.39 = f32[8,4,1,8,256]{4,3,1,2,0:T(8,128)} fusion(f32[8,4,1,8,256]{4,3,1,2,0:T(8,128)} %fusion.40, f32[4,8,8,256]{3,2,0,1:T(8,128)S(1)} %fusion.13), kind=kLoop, calls=%fused_computation.75 | loop fusion | bytes 65536
  14.8 0.6 %fusion.38 = f32[8,4,1,8,256]{4,3,1,2,0:T(8,128)} fusion(f32[8,4,1,8,256]{4,3,1,2,0:T(8,128)} %fusion.39, f32[4,8,8,256]{3,2,0,1:T(8,128)S(1)} %fusion.13), kind=kLoop, calls=%fused_computation.73 | loop fusion | bytes 65536
  15.4 0.6 %fusion.37 = f32[8,4,1,8,256]{4,3,1,2,0:T(8,128)} fusion(f32[8,4,1,8,256]{4,3,1,2,0:T(8,128)} %fusion.38, f32[4,8,8,256]{3,2,0,1:T(8,128)S(1)} %fusion.13), kind=kLoop, calls=%fused_computation.71 | loop fusion | bytes 65536
  16.0 0.6 %fusion.36 = f32[8,4,1,8,256]{4,3,1,2,0:T(8,128)} fusion(f32[8,4,1,8,256]{4,3,1,2,0:T(8,128)} %fusion.37, f32[4,8,8,256]{3,2,0,1:T(8,128)S(1)} %fusion.13), kind=kLoop, calls=%fused_computation.69 | loop fusion | bytes 65536
  16.6 0.6 %fusion.35 = f32[8,4,1,8,256]{4,3,1,2,0:T(8,128)} fusion(f32[8,4,1,8,256]{4,3,1,2,0:T(8,128)} %fusion.36, f32[4,8,8,256]{3,2,0,1:T(8,128)S(1)} %fusion.13), kind=kLoop, calls=%fused_computation.67 | loop fusion | bytes 65536
  17.3 0.6 %fusion.34 = f32[8,4,1,8,256]{4,3,1,2,0:T(8,128)} fusion(f32[8,4,1,8,256]{4,3,1,2,0:T(8,128)} %fusion.35, f32[4,8,8,256]{3,2,0,1:T(8,128)S(1)} %fusion.13), kind=kLoop, calls=%fused_computation.65 | loop fusion | bytes 65536
  17.9 0.6 %fusion.33 = f32[8,4,1,8,256]{4,3,1,2,0:T(8,128)} fusion(f32[8,4,1,8,256]{4,3,1,2,0:T(8,128)} %fusion.34, f32[4,8,8,256]{3,2,0,1:T(8,128)S(1)} %fusion.13), kind=kLoop, calls=%fused_computation.63 | loop fusion | bytes 65536 | tf_op jit(solution)/shard_map/stack | solution.py:12
  18.5 3.7 %all-to-all-start = ((f32[8,4,1,8,256]{4,3,1,2,0:T(8,128)}), f32[8,4,1,8,256]{4,3,1,2,0:T(8,128)S(1)}, u32[]{:S(2)}, u32[]{:S(2)}) async-start(f32[8,4,1,8,256]{4,3,1,2,0:T(8,128)} %fusion.33), calls=%async_computation | async-start | bytes 524288 | tf_op jit(solution)/shard_map/all_to_all | solution.py:13
  22.2 0.7 %compare_and_fusion = pred[8,128]{1,0:T(8,128)(4,1)S(1)} fusion(s32[64,128]{1,0:T(8,128)} %bitcast.115, s32[]{:T(128)S(6)} %select_n.18), kind=kLoop, calls=%fused_computation.88 | loop fusion | flops 6144 | bytes 5124 | tf_op jit(solution)/shard_map/vmap(jit(_take))/and | solution.py:71
  22.9 6.2 %all-to-all-done = f32[8,4,1,8,256]{4,3,1,2,0:T(8,128)S(1)} async-done(((f32[8,4,1,8,256]{4,3,1,2,0:T(8,128)}), f32[8,4,1,8,256]{4,3,1,2,0:T(8,128)S(1)}, u32[]{:S(2)}, u32[]{:S(2)}) %all-to-all-start) | async-done | bytes 262176 | tf_op jit(solution)/shard_map/all_to_all | solution.py:13
  29.1 0.4 copy.33
  29.5 6.8 %gather_fusion = f32[1024,32]{1,0:T(8,128)S(1)} fusion(f32[8,32,256]{1,2,0:T(8,128)S(1)} %bitcast.101, s32[1024]{0:T(1024)S(1)} %fusion.45), kind=kCustom, calls=%fused_computation | custom fusion | bytes 270336 | tf_op jit(solution)/shard_map/vmap(jit(_take))/gather | solution.py:71
  36.5 0.7 %subtract_multiply_fusion = (f32[8,128]{1,0:T(8,128)S(1)}, f32[8,128]{1,0:T(8,128)S(1)}, f32[8,128]{1,0:T(8,128)S(1)}) fusion(f32[64,128]{1,0:T(8,128)} %bitcast.116, s32[]{:T(128)S(6)} %select_n.18, f32[64,128]{1,0:T(8,128)} %bitcast.117, f32[8,128]{1,0:T(8,128)S(1)} %bitcast_reduce_fusion), kind=kLoop, calls=%fused_computation.86 | loop fusion | flops 3072 | bytes 24580 | tf_op jit(solution)/shard_map/mul | solution.py:61
  37.2 0.4 multiply_reduce_fusion
  37.7 0.3 fusion.3
  40.9 0.5 fusion
  41.6 9.3 %all_to_all.23 = f32[32,1,8,256]{3,2,1,0:T(8,128)S(1)} all-to-all(f32[32,1,8,256]{3,2,1,0:T(8,128)S(1)} %copy.37), channel_id=1, replica_groups=mesh['member'=8,'lat'=4] {'member'}, dimensions={0} | all-to-all | bytes 524288 | tf_op jit(solution)/shard_map/all_to_all | solution.py:97
  50.9 0.7 %copy.55 = f32[8,4,1,8,256]{4,3,0,1,2:T(8,128)} copy(f32[8,4,1,8,256]{4,3,1,0,2:T(8,128)S(1)} %bitcast.110) | data formatting | bytes 524288 | tf_op jit(solution)/shard_map/all_to_all | solution.py:97
  (35 shorter events, 4.4 us)
Async XLA Ops:
  0.0 12.5 %copy-start = (f32[4,8,8,256]{3,2,1,0:T(8,128)S(1)}, f32[4,8,8,256]{3,2,1,0:T(8,128)}, u32[]{:S(2)}) copy-start(f32[4,8,8,256]{3,2,1,0:T(8,128)} %param.6) | copy-start | bytes 786436
  0.0 12.5 %copy-start.1 = (f32[8,8,256]{2,1,0:T(8,128)S(1)}, f32[8,8,256]{2,1,0:T(8,128)}, u32[]{:S(2)}) copy-start(f32[8,8,256]{2,1,0:T(8,128)} %param.8) | copy-start | bytes 196612
  0.0 12.5 %copy-start.2 = (f32[8,8,256]{2,1,0:T(8,128)S(1)}, f32[8,8,256]{2,1,0:T(8,128)}, u32[]{:S(2)}) copy-start(f32[8,8,256]{2,1,0:T(8,128)} %param.7) | copy-start | bytes 196612
  1.0 7.2 %collective-permute-start = (f32[6,2,8,256]{3,2,0,1:T(8,128)S(1)}, f32[6,2,8,256]{3,2,0,1:T(8,128)S(1)}, u32[]{:S(2)}, u32[]{:S(2)}) collective-permute-start(f32[6,2,8,256]{3,2,0,1:T(8,128)S(1)} %get-tuple-element.12), channel_id=1, source_target_pairs={{0,1},{1,2},{2,3},{4,5},{5,6},{6,7},{8,9},{9,10},{10,11},{12,13},{... | collective-permute-start | bytes 294920 | tf_op jit(solution)/shard_map/ppermute | solution.py:22
  6.0 6.5 %collective-permute-start.1 = (f32[6,2,8,256]{3,2,0,1:T(8,128)S(1)}, f32[6,2,8,256]{3,2,0,1:T(8,128)S(1)}, u32[]{:S(2)}, u32[]{:S(2)}) collective-permute-start(f32[6,2,8,256]{3,2,0,1:T(8,128)S(1)} %get-tuple-element.11), channel_id=1, source_target_pairs={{1,0},{2,1},{3,2},{5,4},{6,5},{7,6},{9,8},{10,9},{11,10},{13,12},{... | collective-permute-start | bytes 294920 | tf_op jit(solution)/shard_map/ppermute | solution.py:25
  18.5 10.6 %all-to-all-start = ((f32[8,4,1,8,256]{4,3,1,2,0:T(8,128)}), f32[8,4,1,8,256]{4,3,1,2,0:T(8,128)S(1)}, u32[]{:S(2)}, u32[]{:S(2)}) async-start(f32[8,4,1,8,256]{4,3,1,2,0:T(8,128)} %fusion.33), calls=%async_computation | async-start | bytes 524288 | tf_op jit(solution)/shard_map/all_to_all | solution.py:13
